TPU v7x, 32 devices: a whole 2x2x4 slice. The times are simulated.
32 devices in a mesh: group: 4 (over x, core), tensor: 4 (over z), dp: 2 (over y).
Axes of the slice: x: 2, y: 2, z: 4, core: 2. Of those that a mesh axis runs over, the one named last changes fastest.
Arguments:
- doc_emb: bfloat16 [48, 4096], P('group', 'dp'), may hold values from -6 to 6
- row_emb: bfloat16 [64, 4096], P(None, 'dp'), may hold values from -6 to 6
- hyper_in: bfloat16 [4096, 8192], P('dp', 'tensor'), may hold values from -0.09375 to 0.09375
- hyper_out: bfloat16 [8192, 8192], P('tensor', 'dp'), may hold values from -0.0625 to 0.0625
- assign: int32 [48], replicated, may hold values from 0 to 47, each once
- states: bfloat16 [2304, 8192], P('group', 'tensor'), may hold values from -6 to 6
- proj_weight: bfloat16 [8192, 8192], P('tensor', 'dp'), may hold values from -0.0625 to 0.0625
- targets: bfloat16 [2304, 8192], P(('group', 'tensor'), 'dp'), may hold values from -6 to 6
Outputs:
- adapted: bfloat16 [2304, 8192], P(('group', 'tensor'), 'dp')
- grad_down: float32 [48, 32, 8192], P('group', None, 'tensor')
- grad_up: float32 [48, 32, 8192], P('group', None, ('dp', 'tensor'))
Inputs may be any that keep to these rules, and one draw needn't show every extreme that they name: `assign`: every document is named by exactly one slot.
All inputs are finite; a program needn't handle non-finite values.
Results may differ from a plain program's by a relative error of at most 0.02.
Values may be sent and summed in bfloat16 or wider, within the bound.
No kernel may reach another device: no remote copies, remote signals or barrier semaphores. Data moves between devices by JAX's collectives and lax.ppermute only.
A program may use at most 128 MiB of HBM per device.

v0:
```python
import math
import jax
import jax.numpy as jnp
from jax import lax
from jax.sharding import PartitionSpec as P

D = 8192
R = 32
LOWDIM_MULTIPLE = 0.1


def spread(block, axis, owner):
    block = jnp.where(lax.axis_index(axis) == owner, block, jnp.zeros_like(block))
    return lax.psum(block, axis)


def hypernet(doc_rows, row_emb, hyper_in, hyper_out):
    doc_count = doc_rows.shape[0]
    pre_doc, pre_row = (
        lax.psum(
            jnp.dot(doc_rows, hyper_in, preferred_element_type=jnp.float32).astype(jnp.bfloat16),
            "dp",
        ).astype(jnp.float32),
        lax.psum(
            jnp.dot(row_emb, hyper_in, preferred_element_type=jnp.float32).astype(jnp.bfloat16),
            "dp",
        ).astype(jnp.float32),
    )
    hidden = jax.nn.silu(pre_doc[:, None, :] + pre_row[None, :, :]).astype(jnp.bfloat16)
    hidden = hidden.reshape(doc_count * 2 * R, hidden.shape[2])
    partial_value = jnp.dot(hidden, hyper_out, preferred_element_type=jnp.float32)
    summed = lax.psum(partial_value.astype(jnp.bfloat16), "tensor")
    factors = summed.reshape(doc_count, 2 * R, hyper_out.shape[1])
    ratio_axes = lax.axis_size("tensor") // lax.axis_size("dp")
    owner_rows = spread(factors[:, :R, :], "dp", lax.axis_index("tensor") // ratio_axes)
    col_width = hyper_out.shape[1] // ratio_axes
    down_block = lax.dynamic_slice_in_dim(
        owner_rows, lax.axis_index("tensor") % ratio_axes * col_width, col_width, 2
    )
    return (down_block, factors[:, R:, :])


def body(doc_emb, row_emb, hyper_in, hyper_out, assign, states, proj_weight, targets):
    doc_count = doc_emb.shape[0]
    group_start = lax.axis_index("group") * doc_count
    slot_docs = lax.dynamic_slice_in_dim(assign, group_start, doc_count)
    everyone = lax.all_gather(doc_emb, "group", axis=0, tiled=True)
    picker = (slot_docs[:, None] == jnp.arange(everyone.shape[0], dtype=jnp.int32)[None, :]).astype(
        jnp.bfloat16
    )
    chosen = jnp.dot(picker, everyone, preferred_element_type=jnp.float32).astype(jnp.bfloat16)
    slot_down, slot_up_factor = hypernet(chosen, row_emb, hyper_in, hyper_out)
    token_count = states.shape[0]
    per_doc = token_count // doc_count
    fan_width_multiplier = 1.0 / math.sqrt(D)
    bundled_entries = states.reshape(doc_count, per_doc, states.shape[1])
    low_part = jnp.einsum(
        "quw,qlw->qul", bundled_entries, slot_down, preferred_element_type=jnp.float32
    ).reshape(token_count, R)
    base_part = jnp.dot(states, proj_weight, preferred_element_type=jnp.float32)
    frozen_output, low_sum = (
        lax.psum_scatter(
            base_part.astype(jnp.bfloat16), "tensor", scatter_dimension=0, tiled=True
        ).astype(jnp.float32),
        lax.psum_scatter(
            low_part.astype(jnp.bfloat16), "tensor", scatter_dimension=0, tiled=True
        ).astype(jnp.float32),
    )
    row_count = frozen_output.shape[0]
    row_start = lax.axis_index("tensor") * row_count
    owner_doc = (row_start + jnp.arange(row_count, dtype=jnp.int32)) // per_doc
    document_member = owner_doc[:, None] == jnp.arange(doc_count, dtype=jnp.int32)[None, :]
    narrow_basis_map = (low_sum * fan_width_multiplier).astype(jnp.bfloat16)
    broadcast_rows = jnp.where(
        document_member[:, :, None], narrow_basis_map[:, None, :], jnp.zeros((), jnp.bfloat16)
    ).reshape(row_count, doc_count * R)
    up_factor_rows = slot_up_factor.reshape(doc_count * R, slot_up_factor.shape[2])
    raised_rows = frozen_output + LOWDIM_MULTIPLE * jnp.dot(
        broadcast_rows, up_factor_rows, preferred_element_type=jnp.float32
    )
    adapted = raised_rows.astype(jnp.bfloat16)
    residual = (raised_rows - targets.astype(jnp.float32)).astype(jnp.bfloat16)
    partial_up_gradient = LOWDIM_MULTIPLE * lax.dot_general(
        broadcast_rows, residual, (((0,), (0,)), ((), ())), preferred_element_type=jnp.float32
    )
    grad_up_local = lax.psum_scatter(
        partial_up_gradient.reshape(doc_count, R, up_factor_rows.shape[1]).astype(jnp.bfloat16),
        "tensor",
        scatter_dimension=2,
        tiled=True,
    ).astype(jnp.float32)
    document_list = lax.dot_general(
        residual, up_factor_rows, (((1,), (1,)), ((), ())), preferred_element_type=jnp.float32
    ).reshape(row_count, doc_count, R)
    token_portion = LOWDIM_MULTIPLE * jnp.sum(
        jnp.where(document_member[:, :, None], document_list, 0.0), axis=1
    )
    placed = lax.dynamic_update_slice_in_dim(
        jnp.zeros((token_count, R), jnp.float32), token_portion, row_start, 0
    )
    position_sensitivity = lax.psum(placed, ("tensor", "dp")).astype(jnp.bfloat16)
    lowering_matrix_sensitivity = fan_width_multiplier * jnp.einsum(
        "oed,oec->odc",
        position_sensitivity.reshape(doc_count, per_doc, R),
        bundled_entries,
        preferred_element_type=jnp.float32,
    )
    own_docs = group_start + jnp.arange(doc_count, dtype=jnp.int32)
    initial_grads = (
        jnp.zeros(
            (
                doc_count,
                lowering_matrix_sensitivity.shape[1] * lowering_matrix_sensitivity.shape[2],
            ),
            jnp.float32,
        ),
        jnp.zeros((doc_count, grad_up_local.shape[1] * grad_up_local.shape[2]), jnp.float32),
    )
    pieces = (
        lax.all_gather(
            lowering_matrix_sensitivity.astype(jnp.bfloat16), "group", axis=0, tiled=True
        ).astype(jnp.float32),
        lax.all_gather(grad_up_local.astype(jnp.bfloat16), "group", axis=0, tiled=True).astype(
            jnp.float32
        ),
    )
    piece_rows = pieces[0].shape[0]
    picker = (own_docs[:, None] == assign[None, :]).astype(jnp.float32)
    first = initial_grads[0] + jnp.dot(
        picker, pieces[0].reshape(piece_rows, -1), precision=lax.Precision.HIGHEST
    )
    second = initial_grads[1] + jnp.dot(
        picker, pieces[1].reshape(piece_rows, -1), precision=lax.Precision.HIGHEST
    )
    grad_down = first.reshape(lowering_matrix_sensitivity.shape)
    grad_up = second.reshape(grad_up_local.shape)
    return (adapted, grad_down, grad_up)


def solution(mesh):
    in_specs = (
        P("group", "dp"),
        P(None, "dp"),
        P("dp", "tensor"),
        P("tensor", "dp"),
        P(),
        P("group", "tensor"),
        P("tensor", "dp"),
        P(("group", "tensor"), "dp"),
    )
    out_specs = (
        P(("group", "tensor"), "dp"),
        P("group", None, "tensor"),
        P("group", None, ("dp", "tensor")),
    )
    return jax.shard_map(body, mesh=mesh, in_specs=in_specs, out_specs=out_specs, check_vma=False)
```

profile of v0, /device:TPU:0, one launch (start us, length us, event | category | flops | bytes accessed | tf_op | source)
XLA Modules:
  0.0 643.9 jit_solution(16494009230367694234)
XLA Ops:
  7.2 5.9 convolution_convert_fusion.2
  13.2 7.2 %all-gather = bf16[4,12,2048]{2,1,0:T(8,128)(2,1)S(1)} all-gather(bf16[1,12,2048]{2,1,0:T(8,128)(2,1)S(1)} %bitcast.83), channel_id=1, replica_groups=mesh['group'=4,'tensor'=4,'dp'=2] {'group'}, dimensions={0}, use_global_device_ids=true | all-gather | bytes 245760 | tf_op jit(solution)/shard_map/all_gather | solution.py:47
  20.6 4.8 convolution_convert_fusion.4
  25.4 8.9 %psum.35 = bf16[12,2048]{1,0:T(8,128)(2,1)S(1)} all-reduce(bf16[12,2048]{1,0:T(8,128)(2,1)S(1)} %convolution_convert_fusion.4), channel_id=1, replica_groups=mesh['group'=4,'tensor'=4,'dp'=2] {'dp'}, use_global_device_ids=true, to_apply=%region_1.0 | all-reduce | flops 24576 | bytes 98304 | tf_op jit(solution)/shard_map/psum | solution.py:20
  34.3 5.0 all-reduce.4.cloned.1.call-done
  42.8 18.5 %convolution_convert_fusion = bf16[768,4096]{1,0:T(8,128)(2,1)} fusion(bf16[768,2048]{1,0:T(8,128)(2,1)S(1)} %fusion.6, bf16[2048,4096]{1,0:T(8,128)(2,1)} %param.11), kind=kOutput, calls=%fused_computation | convolution fusion | flops 12888047616 | bytes 26214400 | tf_op jit(solution)/shard_map/dot_general | solution.py:31
  61.4 222.9 %all-reduce.6.cloned.1.call-done = bf16[12,64,4096]{2,1,0:T(8,128)(2,1)} async-done(((bf16[12,64,4096]{2,1,0:T(8,128)(2,1)}), bf16[12,64,4096]{2,1,0:T(8,128)(2,1)}) %all-reduce.6.cloned.1.call-update) | async-done | bytes 6291472 | tf_op jit(solution)/shard_map/psum | solution.py:32
  284.4 3.8 slice_select_fusion
  288.2 84.8 %all-reduce.8.cloned.1.call-done = bf16[12,32,4096]{2,1,0:T(8,128)(2,1)} async-done(((bf16[12,32,4096]{2,1,0:T(8,128)(2,1)}), bf16[12,32,4096]{2,1,0:T(8,128)(2,1)}) %all-reduce.8.cloned.1.call-update) | async-done | bytes 3145744 | tf_op jit(solution)/shard_map/psum | solution.py:14
  373.0 2.1 fusion.31
  376.2 15.0 %convolution_convert_fusion.1 = bf16[576,4096]{1,0:T(8,128)(2,1)} fusion(bf16[576,2048]{1,0:T(8,128)(2,1)S(1)} %copy-done, bf16[2048,4096]{1,0:T(8,128)(2,1)} %param.14), kind=kOutput, calls=%fused_computation.11 | convolution fusion | flops 9666035712 | bytes 23855104 | tf_op jit(solution)/shard_map/dot_general | solution.py:60
  391.3 4.4 reduce-scatter.10.cloned.1.call-done
  397.2 84.1 %reduce-scatter.6.cloned.1.call-done = bf16[144,4096]{1,0:T(8,128)(2,1)} async-done(((bf16[576,4096]{1,0:T(8,128)(2,1)}), bf16[144,4096]{1,0:T(8,128)(2,1)}) %reduce-scatter.6.cloned.1.call-update) | async-done | bytes 1179664 | tf_op jit(solution)/shard_map/reduce_scatter | solution.py:62
  481.4 4.1 fusion.47
  485.5 2.7 multiply_convert_fusion
  488.8 3.6 fusion.23
  492.9 40.6 %psum.39 = bf16[576,32]{0,1:T(8,128)(2,1)S(1)} all-reduce(f32[576,32]{0,1:T(8,128)S(1)} %dynamic_update_slice.3), channel_id=1, replica_groups=mesh['group'=4,'tensor'=4,'dp'=2] {'tensor','dp'}, use_global_device_ids=true, to_apply=%region_7.8 | all-reduce | flops 18432 | bytes 110592 | tf_op jit(solution)/shard_map/psum | solution.py:101
  535.7 15.1 %reduce-scatter.8.cloned.1.call-done = bf16[12,32,1024]{2,1,0:T(8,128)(2,1)} async-done(((bf16[12,32,4096]{2,1,0:T(8,128)(2,1)}), bf16[12,32,1024]{2,1,0:T(8,128)(2,1)}) %reduce-scatter.8.cloned.1.call-update) | async-done | bytes 786448 | tf_op jit(solution)/shard_map/reduce_scatter | solution.py:86
  550.8 48.7 %all-gather.4.cloned.1.call-done = bf16[48,32,2048]{2,1,0:T(8,128)(2,1)} async-done(((bf16[12,32,2048]{2,1,0:T(8,128)(2,1)}), bf16[48,32,2048]{2,1,0:T(8,128)(2,1)}) %all-gather.4.cloned.1.call-update) | async-done | bytes 6291472 | tf_op jit(solution)/shard_map/all_gather | solution.py:120
  599.6 9.6 %fusion = f32[12,32,2048]{2,0,1:T(8,128)S(1)} fusion(s32[48]{0:T(128)S(1)} %copy-done.8, s32[12]{0:T(128)S(1)} %iota_add_fusion, bf16[6,8,32,2048]{3,2,1,0:T(8,128)(2,1)} %bitcast.79), kind=kOutput, calls=%fused_computation.1 | convolution fusion | flops 75498048 | bytes 9437424 | tf_op jit(solution)/shard_map/dot_general | solution.py:129
  609.1 3.5 copy.23
  612.6 17.1 %all-gather.6.cloned.1.call-done = bf16[48,32,1024]{2,1,0:T(8,128)(2,1)} async-done(((bf16[12,32,1024]{2,1,0:T(8,128)(2,1)}), bf16[48,32,1024]{2,1,0:T(8,128)(2,1)}) %all-gather.6.cloned.1.call-update) | async-done | bytes 3145744 | tf_op jit(solution)/shard_map/all_gather | solution.py:123
  629.7 5.3 fusion.9
  635.0 2.1 copy.24
  (52 shorter events, 9.8 us)
Async XLA Ops:
  7.2 365.9 %copy-start = (bf16[576,2048]{1,0:T(8,128)(2,1)S(1)}, bf16[576,2048]{1,0:T(8,128)(2,1)}, u32[]{:S(2)}) copy-start(bf16[576,2048]{1,0:T(8,128)(2,1)} %param.13) | copy-start | bytes 7077892
  7.2 6.0 copy-start.4
  7.2 13.3 %copy-start.7 = (s32[48]{0:T(128)S(1)}, s32[48]{0:T(128)}, u32[]{:S(2)}) copy-start(s32[48]{0:T(128)} %param.12) | copy-start | bytes 580
  7.2 32.1 %all-reduce.4.cloned.1.call-start = ((), (), s32[]{:S(2)}) async-start(), calls=%async_computation.4 | async-start | bytes 524288 | tf_op jit(solution)/shard_map/psum | solution.py:24
  13.2 271.2 %all-reduce.6.cloned.1.call-start = ((), (), s32[]{:S(2)}) async-start(), calls=%async_computation.5 | async-start | bytes 12582912 | tf_op jit(solution)/shard_map/psum | solution.py:32
  61.4 311.7 %all-reduce.8.cloned.1.call-start = ((), (), s32[]{:S(2)}) async-start(), calls=%async_computation.6 | async-start | bytes 6291456 | tf_op jit(solution)/shard_map/psum | solution.py:14
  288.1 107.5 %reduce-scatter.10.cloned.1.call-start = ((), (), s32[]{:S(2)}) async-start(), calls=%async_computation.10 | async-start | bytes 184320
  376.0 105.4 %reduce-scatter.6.cloned.1.call-start = ((), (), s32[]{:S(2)}) async-start(), calls=%async_computation.3 | async-start | bytes 5898240 | tf_op jit(solution)/shard_map/reduce_scatter | solution.py:62
  391.2 159.6 %reduce-scatter.8.cloned.1.call-start = ((), (), s32[]{:S(2)}) async-start(), calls=%async_computation.8 | async-start | bytes 3932160 | tf_op jit(solution)/shard_map/reduce_scatter | solution.py:86
  391.3 5.3 copy-start.5
  397.2 88.2 %copy-start.2 = (bf16[144,4096]{1,0:T(8,128)(2,1)S(1)}, bf16[144,4096]{1,0:T(8,128)(2,1)}, u32[]{:S(2)}) copy-start(bf16[144,4096]{1,0:T(8,128)(2,1)} %param.15) | copy-start | bytes 3538948
  481.4 4.1 copy-start.3
  485.5 2.7 copy-start.1
  488.2 0.7 copy-start.6
  488.2 111.4 %all-gather.4.cloned.1.call-start = ((), (), s32[]{:S(2)}) async-start(), calls=%async_computation.7 | async-start | bytes 7864320 | tf_op jit(solution)/shard_map/all_gather | solution.py:120
  533.7 65.9 %copy-start.8 = (s32[48]{0:T(128)S(1)}, s32[48]{0:T(128)}, u32[]{:S(2)}) copy-start(s32[48]{0:T(128)} %param.12) | copy-start | bytes 580
  535.4 94.2 %all-gather.6.cloned.1.call-start = ((), (), s32[]{:S(2)}) async-start(), calls=%async_computation.9 | async-start | bytes 3932160 | tf_op jit(solution)/shard_map/all_gather | solution.py:123
Sparse Core Ops, SparseCore 0:
  13.3 26.0 all-reduce.3
  61.5 222.8 all-reduce.5
  288.3 84.7 all-reduce.7
  376.1 19.5 reduce-scatter.9
  397.8 83.4 reduce-scatter.5
  488.3 62.4 reduce-scatter.7
  552.9 46.5 all-gather.3
  601.1 28.4 all-gather.5
where the time goes:
time: 644 us
  waiting for transfers between devices  482 us (75%)
  matrix products  73.3 us (11%)
  blocking collectives  56.7 us (9%)
  between operations  14.4 us (2%)
  local copies, waits for them, and re-layouts  8.55 us (1%)
  other arithmetic  7.99 us (1%)
    psum x1, waiting for transfers between devices, hypernet(): summed = lax.psum(partial_value.astype(jnp.bfloat16), 'tensor')  223 us
    psum x1, waiting for transfers between devices, spread(): return lax.psum(block, axis)  84.8 us
    reduce_scatter x1, waiting for transfers between devices, body(): lax.psum_scatter(base_part.astype(jnp.bfloat16), 'tensor', scatter_dimens...  84.1 us
    all_gather x1, waiting for transfers between devices, body(): lax.all_gather(lowering_matrix_sensitivity.astype(jnp.bfloat16), 'group',...  48.7 us
    psum x1, blocking collectives, body(): lax.psum(placed, ('tensor', 'dp')).astype(jnp.bfloat16)  40.6 us
    dot_general x1, matrix products, hypernet(): jnp.dot(hidden, hyper_out, preferred_element_type=jnp.float32)  18.5 us
    all_gather x1, waiting for transfers between devices, body(): lax.all_gather(grad_up_local.astype(jnp.bfloat16), 'group', axis=0, tiled...  17.1 us
    reduce_scatter x1, waiting for transfers between devices, body(): lax.psum_scatter(partial_up_gradient.reshape(doc_count, R, up_factor_rows...  15.1 us
  transfers between devices with their start and end apart: 8, of which 8 were waited for; matrix products, arithmetic and copies ran while one was open for 6% of the time, Pallas kernels for 0%

commit v1 on v0

--- a/solution.py
+++ b/solution.py
@@ -98,7 +98,7 @@
     placed = lax.dynamic_update_slice_in_dim(
         jnp.zeros((token_count, R), jnp.float32), token_portion, row_start, 0
     )
-    position_sensitivity = lax.psum(placed, ("tensor", "dp")).astype(jnp.bfloat16)
+    position_sensitivity = lax.psum(lax.psum(placed, "dp"), "tensor").astype(jnp.bfloat16)
     lowering_matrix_sensitivity = fan_width_multiplier * jnp.einsum(
         "oed,oec->odc",
         position_sensitivity.reshape(doc_count, per_doc, R),

time: 644 us -> 671 us (1.042)
  waiting for transfers between devices: 482 us -> 524 us
  blocking collectives: 56.7 us -> 38.4 us
    reduce_scatter x1, waiting for transfers between devices: 15.1 us -> 39.6 us  [body(): lax.psum_scatter(partial_up_gradient.reshape(doc_count, R, up_factor_rows...]
    psum x1, blocking collectives: 40.6 us -> 22.3 us  [body(): lax.psum(lax.psum(placed, 'dp'), 'tensor').astype(jnp.bfloat16)]
    psum x0 -> x1, waiting for transfers between devices: none -> 17.3 us  [body(): lax.psum(placed, 'dp')]
  transfers between devices with their start and end apart: 8 -> 9, of which waited for: 8 -> 9; matrix products, arithmetic and copies ran while one was open for 6% -> 6% of each run, Pallas kernels for 0% -> 0%
where the time goes in v1:
time: 671 us
  waiting for transfers between devices  524 us (78%)
  matrix products  75.2 us (11%)
  blocking collectives  38.4 us (6%)
  between operations  14.1 us (2%)
  local copies, waits for them, and re-layouts  9.54 us (1%)
  other arithmetic  8.6 us (1%)
    psum x1, waiting for transfers between devices, hypernet(): summed = lax.psum(partial_value.astype(jnp.bfloat16), 'tensor')  223 us
    psum x1, waiting for transfers between devices, spread(): return lax.psum(block, axis)  84.8 us
    reduce_scatter x1, waiting for transfers between devices, body(): lax.psum_scatter(base_part.astype(jnp.bfloat16), 'tensor', scatter_dimens...  84.1 us
    all_gather x1, waiting for transfers between devices, body(): lax.all_gather(lowering_matrix_sensitivity.astype(jnp.bfloat16), 'group',...  48.7 us
    reduce_scatter x1, waiting for transfers between devices, body(): lax.psum_scatter(partial_up_gradient.reshape(doc_count, R, up_factor_rows...  39.6 us
    psum x1, blocking collectives, body(): lax.psum(lax.psum(placed, 'dp'), 'tensor').astype(jnp.bfloat16)  22.3 us
    dot_general x1, matrix products, hypernet(): jnp.dot(hidden, hyper_out, preferred_element_type=jnp.float32)  18.5 us
    psum x1, waiting for transfers between devices, body(): lax.psum(placed, 'dp')  17.3 us
  transfers between devices with their start and end apart: 9, of which 9 were waited for; matrix products, arithmetic and copies ran while one was open for 6% of the time, Pallas kernels for 0%

profile of v1, /device:TPU:0, one launch (start us, length us, event | category | flops | bytes accessed | tf_op | source)
XLA Modules:
  0.0 670.7 jit_solution(14541440390857032090)
XLA Ops:
  7.2 5.9 convolution_convert_fusion.2
  13.2 7.2 %all-gather = bf16[4,12,2048]{2,1,0:T(8,128)(2,1)S(1)} all-gather(bf16[1,12,2048]{2,1,0:T(8,128)(2,1)S(1)} %bitcast.83), channel_id=1, replica_groups=mesh['group'=4,'tensor'=4,'dp'=2] {'group'}, dimensions={0}, use_global_device_ids=true | all-gather | bytes 245760 | tf_op jit(solution)/shard_map/all_gather | solution.py:47
  20.6 4.8 convolution_convert_fusion.4
  25.4 8.9 %psum.42 = bf16[12,2048]{1,0:T(8,128)(2,1)S(1)} all-reduce(bf16[12,2048]{1,0:T(8,128)(2,1)S(1)} %convolution_convert_fusion.4), channel_id=1, replica_groups=mesh['group'=4,'tensor'=4,'dp'=2] {'dp'}, use_global_device_ids=true, to_apply=%region_1.0 | all-reduce | flops 24576 | bytes 98304 | tf_op jit(solution)/shard_map/psum | solution.py:20
  34.3 5.0 all-reduce.5.cloned.1.call-done
  42.8 18.5 %convolution_convert_fusion = bf16[768,4096]{1,0:T(8,128)(2,1)} fusion(bf16[768,2048]{1,0:T(8,128)(2,1)S(1)} %fusion.6, bf16[2048,4096]{1,0:T(8,128)(2,1)} %param.11), kind=kOutput, calls=%fused_computation | convolution fusion | flops 12888047616 | bytes 26214400 | tf_op jit(solution)/shard_map/dot_general | solution.py:31
  61.4 222.9 %all-reduce.7.cloned.1.call-done = bf16[12,64,4096]{2,1,0:T(8,128)(2,1)} async-done(((bf16[12,64,4096]{2,1,0:T(8,128)(2,1)}), bf16[12,64,4096]{2,1,0:T(8,128)(2,1)}) %all-reduce.7.cloned.1.call-update) | async-done | bytes 6291472 | tf_op jit(solution)/shard_map/psum | solution.py:32
  284.3 3.8 slice_select_fusion
  288.2 84.8 %all-reduce.9.cloned.1.call-done = bf16[12,32,4096]{2,1,0:T(8,128)(2,1)} async-done(((bf16[12,32,4096]{2,1,0:T(8,128)(2,1)}), bf16[12,32,4096]{2,1,0:T(8,128)(2,1)}) %all-reduce.9.cloned.1.call-update) | async-done | bytes 3145744 | tf_op jit(solution)/shard_map/psum | solution.py:14
  373.0 2.1 fusion.31
  376.2 15.0 %convolution_convert_fusion.1 = bf16[576,4096]{1,0:T(8,128)(2,1)} fusion(bf16[576,2048]{1,0:T(8,128)(2,1)S(1)} %copy-done, bf16[2048,4096]{1,0:T(8,128)(2,1)} %param.14), kind=kOutput, calls=%fused_computation.11 | convolution fusion | flops 9666035712 | bytes 23855104 | tf_op jit(solution)/shard_map/dot_general | solution.py:60
  391.3 4.4 reduce-scatter.10.cloned.1.call-done
  397.2 84.1 %reduce-scatter.6.cloned.1.call-done = bf16[144,4096]{1,0:T(8,128)(2,1)} async-done(((bf16[576,4096]{1,0:T(8,128)(2,1)}), bf16[144,4096]{1,0:T(8,128)(2,1)}) %reduce-scatter.6.cloned.1.call-update) | async-done | bytes 1179664 | tf_op jit(solution)/shard_map/reduce_scatter | solution.py:62
  481.3 4.1 fusion.47
  485.4 3.8 fusion.23
  492.0 4.4 multiply_convert_fusion
  496.5 17.3 %all-reduce.11.cloned.1.call-done = f32[576,32]{0,1:T(8,128)} async-done(((f32[576,32]{0,1:T(8,128)}), f32[576,32]{0,1:T(8,128)}) %all-reduce.11.cloned.1.call-update) | async-done | bytes 73744 | tf_op jit(solution)/shard_map/psum | solution.py:101
  513.8 22.3 %psum.47 = bf16[576,32]{0,1:T(8,128)(2,1)S(1)} all-reduce(f32[576,32]{0,1:T(8,128)} %all-reduce.11.cloned.1.call-done), channel_id=1, replica_groups=mesh['group'=4,'tensor'=4,'dp'=2] {'tensor'}, use_global_device_ids=true, to_apply=%region_8.9 | all-reduce | flops 18432 | bytes 110592 | tf_op jit(solution)/shard_map/psum | solution.py:101
  538.3 39.6 %reduce-scatter.8.cloned.1.call-done = bf16[12,32,1024]{2,1,0:T(8,128)(2,1)} async-done(((bf16[12,32,4096]{2,1,0:T(8,128)(2,1)}), bf16[12,32,1024]{2,1,0:T(8,128)(2,1)}) %reduce-scatter.8.cloned.1.call-update) | async-done | bytes 786448 | tf_op jit(solution)/shard_map/reduce_scatter | solution.py:86
  577.9 48.7 %all-gather.4.cloned.1.call-done = bf16[48,32,2048]{2,1,0:T(8,128)(2,1)} async-done(((bf16[12,32,2048]{2,1,0:T(8,128)(2,1)}), bf16[48,32,2048]{2,1,0:T(8,128)(2,1)}) %all-gather.4.cloned.1.call-update) | async-done | bytes 6291472 | tf_op jit(solution)/shard_map/all_gather | solution.py:120
  626.7 9.6 %fusion = f32[12,32,2048]{2,0,1:T(8,128)S(1)} fusion(s32[48]{0:T(128)S(1)} %copy-done.7, s32[12]{0:T(128)S(1)} %iota_add_fusion, bf16[6,8,32,2048]{3,2,1,0:T(8,128)(2,1)} %bitcast.79), kind=kOutput, calls=%fused_computation.1 | convolution fusion | flops 75498048 | bytes 9437424 | tf_op jit(solution)/shard_map/dot_general | solution.py:129
  636.3 3.5 copy.23
  639.7 17.1 %all-gather.6.cloned.1.call-done = bf16[48,32,1024]{2,1,0:T(8,128)(2,1)} async-done(((bf16[12,32,1024]{2,1,0:T(8,128)(2,1)}), bf16[48,32,1024]{2,1,0:T(8,128)(2,1)}) %all-gather.6.cloned.1.call-update) | async-done | bytes 3145744 | tf_op jit(solution)/shard_map/all_gather | solution.py:123
  656.8 5.3 fusion.9
  (53 shorter events, 13.5 us)
Async XLA Ops:
  7.2 365.8 %copy-start = (bf16[576,2048]{1,0:T(8,128)(2,1)S(1)}, bf16[576,2048]{1,0:T(8,128)(2,1)}, u32[]{:S(2)}) copy-start(bf16[576,2048]{1,0:T(8,128)(2,1)} %param.13) | copy-start | bytes 7077892
  7.2 6.0 copy-start.3
  7.2 13.3 %copy-start.6 = (s32[48]{0:T(128)S(1)}, s32[48]{0:T(128)}, u32[]{:S(2)}) copy-start(s32[48]{0:T(128)} %param.12) | copy-start | bytes 580
  7.2 32.1 %all-reduce.5.cloned.1.call-start = ((), (), s32[]{:S(2)}) async-start(), calls=%async_computation.4 | async-start | bytes 524288 | tf_op jit(solution)/shard_map/psum | solution.py:24
  13.2 271.2 %all-reduce.7.cloned.1.call-start = ((), (), s32[]{:S(2)}) async-start(), calls=%async_computation.5 | async-start | bytes 12582912 | tf_op jit(solution)/shard_map/psum | solution.py:32
  61.3 311.7 %all-reduce.9.cloned.1.call-start = ((), (), s32[]{:S(2)}) async-start(), calls=%async_computation.6 | async-start | bytes 6291456 | tf_op jit(solution)/shard_map/psum | solution.py:14
  288.1 107.5 %reduce-scatter.10.cloned.1.call-start = ((), (), s32[]{:S(2)}) async-start(), calls=%async_computation.11 | async-start | bytes 184320
  376.0 105.3 %reduce-scatter.6.cloned.1.call-start = ((), (), s32[]{:S(2)}) async-start(), calls=%async_computation.3 | async-start | bytes 5898240 | tf_op jit(solution)/shard_map/reduce_scatter | solution.py:62
  391.2 122.6 %all-reduce.11.cloned.1.call-start = ((), (), s32[]{:S(2)}) async-start(), calls=%async_computation.7 | async-start | bytes 163840 | tf_op jit(solution)/shard_map/psum | solution.py:101
  391.3 5.3 copy-start.4
  397.2 88.2 %copy-start.2 = (bf16[144,4096]{1,0:T(8,128)(2,1)S(1)}, bf16[144,4096]{1,0:T(8,128)(2,1)}, u32[]{:S(2)}) copy-start(bf16[144,4096]{1,0:T(8,128)(2,1)} %param.15) | copy-start | bytes 3538948
  481.3 4.1 copy-start.5
  485.4 3.8 copy-start.1
  491.9 86.0 %reduce-scatter.8.cloned.1.call-start = ((), (), s32[]{:S(2)}) async-start(), calls=%async_computation.9 | async-start | bytes 3932160 | tf_op jit(solution)/shard_map/reduce_scatter | solution.py:86
  496.4 130.3 %all-gather.4.cloned.1.call-start = ((), (), s32[]{:S(2)}) async-start(), calls=%async_computation.8 | async-start | bytes 7864320 | tf_op jit(solution)/shard_map/all_gather | solution.py:120
  536.2 90.5 %copy-start.7 = (s32[48]{0:T(128)S(1)}, s32[48]{0:T(128)}, u32[]{:S(2)}) copy-start(s32[48]{0:T(128)} %param.12) | copy-start | bytes 580
  538.0 118.8 %all-gather.6.cloned.1.call-start = ((), (), s32[]{:S(2)}) async-start(), calls=%async_computation.10 | async-start | bytes 3932160 | tf_op jit(solution)/shard_map/all_gather | solution.py:123
Sparse Core Ops, SparseCore 0:
  13.3 26.0 all-reduce.4
  61.5 222.8 all-reduce.6
  288.3 84.7 all-reduce.8
  376.1 19.5 reduce-scatter.9
  397.8 83.4 reduce-scatter.5
  492.0 21.7 all-reduce.10
  516.7 61.1 reduce-scatter.7
  580.0 46.6 all-gather.3
  628.3 28.4 all-gather.5
